TPU v7x, 32 devices: a whole 2x2x4 slice. The times are simulated.
32 devices in a mesh: ids: 8 (over z, x), mdl: 4 (over y, core).
Axes of the slice: x: 2, y: 2, z: 4, core: 2. Of those that a mesh axis runs over, the one named last changes fastest.
Arguments:
- hash_codes: int32 [32768, 1024], P('ids', 'mdl'), may hold values from 0 to 1023
- request_ids: int32 [64, 1024], P('ids'), may hold values from 0 to 32767, as said below
- request_counts: int32 [64], P('ids'), may hold values from 256 to 1024, as said below
- token_slots: int32 [65536], P('ids'), may hold values from 0 to 8191, as said below
- cotangent: bfloat16 [65536, 32], P('ids'), may hold values from -6 to 6
- weight_first: float32 [1024, 1800], P('ids', 'mdl'), may hold values from -0.1875 to 0.1875
- weight_second: float32 [1800, 1800], P(None, 'mdl'), may hold values from -0.125 to 0.125
- weight_final: float32 [1800, 32], P('mdl'), may hold values from -0.125 to 0.125
- norm_params: float32 [4, 1800], P(None, 'mdl')
- bias_final: float32 [32], replicated, may hold values from -0.5 to 0.5
- moment_first: float32 [1024, 1800], P('ids', 'mdl'), may hold values from -0.0007324219 to 0.0007324219
- square_first: float32 [1024, 1800], P('ids', 'mdl'), may hold values from 1.373291e-09 to 5.493164e-09
- moment_second: float32 [1800, 1800], P(None, 'mdl'), may hold values from -0.0007324219 to 0.0007324219
- square_second: float32 [1800, 1800], P(None, 'mdl'), may hold values from 1.373291e-09 to 5.493164e-09
- moment_final: float32 [1800, 32], P('mdl'), may hold values from -0.0048828125 to 0.0048828125
- square_final: float32 [1800, 32], P('mdl'), may hold values from 6.103516e-08 to 2.4414064e-07
- moment_norm: float32 [4, 1800], P(None, 'mdl'), may hold values from -0.001953125 to 0.001953125
- square_norm: float32 [4, 1800], P(None, 'mdl'), may hold values from 9e-09 to 3.6e-08
- moment_bias: float32 [32], replicated, may hold values from -0.03125 to 0.03125
- square_bias: float32 [32], replicated, may hold values from 2.5e-06 to 1e-05
Outputs:
- token_embed: bfloat16 [65536, 32], P('ids')
- momentum_first: float32 [1024, 1800], P('ids', 'mdl')
- variance_first: float32 [1024, 1800], P('ids', 'mdl')
- master_first: float32 [1024, 1800], P('ids', 'mdl')
- bfloat_first: bfloat16 [1024, 1800], P('ids', 'mdl')
- momentum_second: float32 [1800, 1800], P(None, 'mdl')
- variance_second: float32 [1800, 1800], P(None, 'mdl')
- master_second: float32 [1800, 1800], P(None, 'mdl')
- bfloat_second: bfloat16 [1800, 1800], P(None, 'mdl')
- momentum_final: float32 [1800, 32], P('mdl')
- variance_final: float32 [1800, 32], P('mdl')
- master_final: float32 [1800, 32], P('mdl')
- bfloat_final: bfloat16 [1800, 32], P('mdl')
- momentum_norm: float32 [4, 1800], P(None, 'mdl')
- variance_norm: float32 [4, 1800], P(None, 'mdl')
- master_norm: float32 [4, 1800], P(None, 'mdl')
- momentum_bias: float32 [32], replicated
- variance_bias: float32 [32], replicated
- master_bias: float32 [32], replicated
Inputs may be any that keep to these rules, and one draw needn't show every extreme that they name: `request_ids`: entries of row s * 8 + j lie in owner j's range j * 4096 to (j + 1) * 4096 - 1; the live ones (the first request_counts of the row) are distinct; the others are padding. `request_counts`: some owner receives exactly 1024 live ids from every device. `token_slots`: each token points at a live slot of its own device, and every live slot of a device is pointed at by one or more of its tokens.
All inputs are finite; a program needn't handle non-finite values.
Results may differ from a plain program's by a relative error of at most 0.003.
The roundings to bfloat16 on the way count: a program that leaves them out, or rounds other values in their place, can miss the bound.
Values may be sent and summed in bfloat16 or wider, within the bound.
A program may use at most 256 MiB of HBM per device.

v0:
```python
import jax
import jax.numpy as jnp
from jax import lax
from jax.sharding import PartitionSpec as P

STEP = 10
beta_one = 0.9
beta_two = 0.999
adam_epsilon = 1e-08
norm_epsilon = 1e-05
penalty_weight = 0.25
decay_matrix = 0.01
rate_matrix = 0.05
rate_norm = 0.5
rate_bias = 0.02
LANES = 128


def mish_parts(inputs):
    grown = jnp.exp(jnp.minimum(inputs, 20.0))
    above = grown * (grown + 2.0)
    inverse = 1.0 / (above + 2.0)
    return (grown, above * inverse, inverse)


def mish(inputs):
    return inputs * mish_parts(inputs)[1]


def mish_slope(inputs):
    grown, gate, inverse = mish_parts(inputs)
    return gate + 4.0 * jnp.minimum(inputs, 20.0) * (grown * inverse) * ((1.0 + grown) * inverse)


def contract(left, right, left_dim, right_dim):
    return lax.dot_general(
        left, right, (((left_dim,), (right_dim,)), ((), ())), preferred_element_type=jnp.float32
    )


def norm_back(upstream, unit_rows, gain_row, scale_row, live_mask, gain_sum, shift_sum, live_count):
    return scale_row * (
        gain_row * upstream
        - live_mask[:, None] * gain_row * (shift_sum + unit_rows * gain_sum) / live_count
    )


def adam(weight, moment, square, gradient, step_rate, shrink):
    momentum = beta_one * moment + (1.0 - beta_one) * gradient
    variance = beta_two * square + (1.0 - beta_two) * gradient * gradient
    moment_hat = momentum / (1.0 - beta_one**STEP)
    square_hat = variance / (1.0 - beta_two**STEP)
    master = weight - step_rate * (
        moment_hat / (jnp.sqrt(square_hat) + adam_epsilon) + shrink * weight
    )
    return (momentum, variance, master)


def split_two(values):
    high = values.astype(jnp.bfloat16)
    low = (values - high.astype(jnp.float32)).astype(jnp.bfloat16)
    return (high, low)


def one_hot(index, length, first):
    rows = lax.broadcasted_iota(jnp.int32, (length, index.shape[0]), 0) + first
    return (rows == index[None, :]).astype(jnp.bfloat16)


def body(
    hash_codes,
    request_ids,
    request_counts,
    token_slots,
    cotangent,
    weight_first,
    weight_second,
    weight_final,
    norm_params,
    bias_final,
    moment_first,
    square_first,
    moment_second,
    square_second,
    moment_final,
    square_final,
    moment_norm,
    square_norm,
    moment_bias,
    square_bias,
):
    owners = lax.axis_size("ids")
    parts = lax.axis_size("mdl")
    part = lax.axis_index("mdl")
    both = ("ids", "mdl")
    range_rows = hash_codes.shape[0]
    rows = range_rows // parts
    slots_per = request_ids.shape[1]
    piece = slots_per // parts
    out_width = weight_final.shape[1]
    width = weight_first.shape[1]
    wide = width + -width % LANES
    hidden = wide * parts
    more = wide - width
    token_count = token_slots.shape[0]
    token_piece = token_count // parts
    token_total = token_count * owners
    first_part = jnp.pad(weight_first.astype(jnp.bfloat16), ((0, 0), (0, more)))
    first_low = lax.all_gather(first_part, "ids", axis=0, tiled=True)
    first_low = lax.all_gather(first_low, "mdl", axis=1, tiled=True)
    second_part = jnp.pad(
        weight_second.astype(jnp.bfloat16).reshape(parts, width, width),
        ((0, 0), (0, more), (0, more)),
    ).reshape(hidden, wide)
    second_low = lax.all_gather(second_part, "mdl", axis=1, tiled=True)
    final_part = jnp.pad(weight_final.astype(jnp.bfloat16), ((0, more), (0, 0)))
    final_low = lax.all_gather(final_part, "mdl", axis=0, tiled=True)
    norm_all = lax.all_gather(jnp.pad(norm_params, ((0, 0), (0, more))), "mdl", axis=1, tiled=True)
    encoded = ((hash_codes.astype(jnp.float32) + 0.5) / 512.0 - 1.0).astype(jnp.bfloat16)
    features = lax.all_to_all(encoded, "mdl", split_axis=0, concat_axis=1, tiled=True)
    owner_row = jnp.arange(owners, dtype=jnp.int32)[:, None]
    wanted = jnp.where(
        jnp.arange(slots_per, dtype=jnp.int32)[None, :] < request_counts[:, None],
        request_ids - owner_row * range_rows,
        range_rows,
    )
    received = lax.all_to_all(wanted, "ids", split_axis=0, concat_axis=0, tiled=True)
    slot_owner = token_slots // slots_per
    slot_place = token_slots % slots_per - part * piece
    slot_here = jnp.where(
        (slot_place >= 0) & (slot_place < piece), slot_owner * piece + slot_place, -1
    )
    slot_sum = (
        jnp.dot(
            one_hot(slot_here, owners * piece, 0), cotangent, preferred_element_type=jnp.float32
        )
        / token_total
    )
    high, low = split_two(slot_sum)
    sent = jnp.concatenate([high, low], axis=1).reshape(owners, piece * 2 * out_width)
    arrived = lax.all_to_all(sent, "ids", split_axis=0, concat_axis=0, tiled=True)
    arrived = lax.all_gather(
        arrived.reshape(owners * piece, 2 * out_width), "mdl", axis=0, tiled=False
    )
    arrived = arrived.reshape(parts * owners * piece, 2 * out_width)
    slot_rows = received.reshape(owners, parts, piece).transpose(1, 0, 2)
    slot_rows = slot_rows.reshape(-1)
    marked = jnp.concatenate(
        [arrived, jnp.ones((arrived.shape[0], 2 * out_width), jnp.bfloat16)], axis=1
    )
    row_sums = jnp.dot(
        one_hot(slot_rows, rows, part * rows), marked, preferred_element_type=jnp.float32
    )
    row_grad = row_sums[:, :out_width] + row_sums[:, out_width : 2 * out_width]
    live_mask = jnp.minimum(row_sums[:, 2 * out_width], 1.0)
    linear_one = jnp.dot(features, first_low, preferred_element_type=jnp.float32)
    active_one = mish(linear_one)
    weighted_one = live_mask[:, None] * active_one
    sums_one = jnp.stack([jnp.sum(weighted_one, 0), jnp.sum(weighted_one * active_one, 0)])
    sums_one, live_count = lax.psum((sums_one, jnp.sum(live_mask)), both)
    mean_one = sums_one[0] / live_count
    scale_one = lax.rsqrt(sums_one[1] / live_count - mean_one * mean_one + norm_epsilon)
    unit_one = (active_one - mean_one) * scale_one
    normed_one = (norm_all[0] * unit_one + norm_all[1]).astype(jnp.bfloat16)
    linear_two = jnp.dot(normed_one, second_low, preferred_element_type=jnp.float32)
    active_two = mish(linear_two)
    weighted_two = live_mask[:, None] * active_two
    sums_two = lax.psum(
        jnp.stack([jnp.sum(weighted_two, 0), jnp.sum(weighted_two * active_two, 0)]), both
    )
    mean_two = sums_two[0] / live_count
    scale_two = lax.rsqrt(sums_two[1] / live_count - mean_two * mean_two + norm_epsilon)
    unit_two = (active_two - mean_two) * scale_two
    normed_two = (norm_all[2] * unit_two + norm_all[3]).astype(jnp.bfloat16)
    embedding = jnp.dot(normed_two, final_low, preferred_element_type=jnp.float32) + bias_final
    embed_low = embedding.astype(jnp.bfloat16)
    embed_range = lax.all_gather(embed_low, "mdl", axis=0, tiled=True)
    slots_mine = lax.dynamic_slice(received, (0, part * piece), (owners, piece)).reshape(-1)
    pick_rows = (
        slots_mine[:, None] == lax.broadcasted_iota(jnp.int32, (owners * piece, range_rows), 1)
    ).astype(jnp.bfloat16)
    replies = jnp.dot(pick_rows, embed_range, preferred_element_type=jnp.float32)
    replies = replies.astype(jnp.bfloat16).reshape(owners, piece * out_width)
    returned = lax.all_to_all(replies, "ids", split_axis=0, concat_axis=0, tiled=True)
    returned = lax.all_gather(returned.reshape(owners, piece, out_width), "mdl", axis=1, tiled=True)
    returned = returned.reshape(owners * slots_per, out_width)
    tokens_mine = lax.dynamic_slice(token_slots, (part * token_piece,), (token_piece,))
    pick_slots = (
        tokens_mine[:, None]
        == lax.broadcasted_iota(jnp.int32, (token_piece, owners * slots_per), 1)
    ).astype(jnp.bfloat16)
    token_part = jnp.dot(pick_slots, returned, preferred_element_type=jnp.float32)
    token_embed = lax.all_gather(token_part.astype(jnp.bfloat16), "mdl", axis=0, tiled=True)
    grad_embed = (
        row_grad + 2.0 * penalty_weight / live_count * live_mask[:, None] * embedding
    ).astype(jnp.bfloat16)
    incoming_two = contract(grad_embed, final_low, 1, 1)
    sums_two = lax.psum(
        jnp.stack([jnp.sum(incoming_two * unit_two, 0), jnp.sum(incoming_two, 0)]), both
    )
    local_final = contract(normed_two, grad_embed, 0, 0)
    local_bias = jnp.sum(grad_embed.astype(jnp.float32), 0)
    outgoing_two = norm_back(
        incoming_two,
        unit_two,
        norm_all[2],
        scale_two,
        live_mask,
        sums_two[0],
        sums_two[1],
        live_count,
    )
    grad_linear_two = (mish_slope(linear_two) * outgoing_two).astype(jnp.bfloat16)
    local_second = jnp.stack(
        [
            contract(normed_one, grad_linear_two[:, wide * k : wide * (k + 1)], 0, 0)
            for k in range(parts)
        ]
    )
    grad_second = lax.psum_scatter(local_second, "mdl", scatter_dimension=0, tiled=False)
    grad_second = lax.psum(grad_second, "ids")
    grad_second = grad_second.reshape(parts, wide, wide)[:, :width, :width].reshape(-1, width)
    incoming_one = contract(grad_linear_two, second_low, 1, 1)
    sums_one, final_sum, grad_bias = lax.psum(
        (
            jnp.stack([jnp.sum(incoming_one * unit_one, 0), jnp.sum(incoming_one, 0)]),
            local_final,
            local_bias,
        ),
        both,
    )
    outgoing_one = norm_back(
        incoming_one,
        unit_one,
        norm_all[0],
        scale_one,
        live_mask,
        sums_one[0],
        sums_one[1],
        live_count,
    )
    grad_linear_one = (mish_slope(linear_one) * outgoing_one).astype(jnp.bfloat16)
    local_first = jnp.stack(
        [
            contract(features, grad_linear_one[:, wide * k : wide * (k + 1)], 0, 0)
            for k in range(parts)
        ]
    )
    grad_first = lax.psum_scatter(local_first, "mdl", scatter_dimension=0, tiled=False)
    grad_first = lax.psum_scatter(grad_first, "ids", scatter_dimension=0, tiled=True)[:, :width]
    start = part * wide
    grad_final = lax.dynamic_slice(final_sum, (start, 0), (width, out_width))
    grad_norm = lax.dynamic_slice(jnp.concatenate([sums_one, sums_two]), (0, start), (4, width))
    momentum_first, variance_first, master_first = adam(
        weight_first, moment_first, square_first, grad_first, rate_matrix, decay_matrix
    )
    momentum_second, variance_second, master_second = adam(
        weight_second, moment_second, square_second, grad_second, rate_matrix, decay_matrix
    )
    momentum_final, variance_final, master_final = adam(
        weight_final, moment_final, square_final, grad_final, rate_matrix, decay_matrix
    )
    momentum_norm, variance_norm, master_norm = adam(
        norm_params, moment_norm, square_norm, grad_norm, rate_norm, 0.0
    )
    momentum_bias, variance_bias, master_bias = adam(
        bias_final, moment_bias, square_bias, grad_bias, rate_bias, 0.0
    )
    return (
        token_embed,
        momentum_first,
        variance_first,
        master_first,
        master_first.astype(jnp.bfloat16),
        momentum_second,
        variance_second,
        master_second,
        master_second.astype(jnp.bfloat16),
        momentum_final,
        variance_final,
        master_final,
        master_final.astype(jnp.bfloat16),
        momentum_norm,
        variance_norm,
        master_norm,
        momentum_bias,
        variance_bias,
        master_bias,
    )


def solution(mesh):
    rows = P("ids", None)
    grid = P("ids", "mdl")
    columns = P(None, "mdl")
    mdl_rows = P("mdl", None)
    return jax.shard_map(
        body,
        mesh=mesh,
        in_specs=(grid, rows, P("ids"), P("ids"), rows, grid, columns, mdl_rows, columns, P())
        + (grid,) * 2
        + (columns,) * 2
        + (mdl_rows,) * 2
        + (columns,) * 2
        + (P(),) * 2,
        out_specs=(rows,)
        + (grid,) * 4
        + (columns,) * 4
        + (mdl_rows,) * 4
        + (columns,) * 3
        + (P(),) * 3,
        check_vma=False,
    )
```

profile of v0, /device:TPU:0, one launch (start us, length us, event | category | flops | bytes accessed | tf_op | source)
XLA Modules:
  0.0 1000.3 jit_solution(2400045335157976259)
XLA Ops:
  9.8 13.0 %subtract_convert_fusion = (bf16[2048,32]{0,1:T(8,128)(2,1)S(1)}, bf16[2048,32]{0,1:T(8,128)(2,1)S(1)}) fusion(bf16[8192,32]{0,1:T(8,128)(2,1)S(1)} %copy-done, s32[8192]{0:T(1024)S(1)} %fusion.37), kind=kOutput, calls=%fused_computation.68 | convolution fusion | flops 1090846720 | bytes 819200 | tf_op jit(solution)/shard_map/dot_general | solution.py:134
  26.4 18.5 %all_to_all.48 = bf16[8,2,8192]{2,1,0:T(2,128)(2,1)S(1)} all-to-all(bf16[8,2,8192]{2,1,0:T(2,128)(2,1)S(1)} %reshape.107), channel_id=1, replica_groups=mesh['ids'=8,'mdl'=4] {'ids'}, dimensions={0} | all-to-all | bytes 524288 | tf_op jit(solution)/shard_map/all_to_all | solution.py:141
  81.7 48.9 %all_gather.27 = f32[4,2048]{1,0:T(4,128)S(1)} all-gather(f32[4,512]{1,0:T(4,128)S(1)} %pad.17), channel_id=1, replica_groups=mesh['ids'=8,'mdl'=4] {'mdl'}, dimensions={1}, use_global_device_ids=true | all-gather | bytes 40960 | tf_op jit(solution)/shard_map/all_gather | solution.py:118
  147.0 11.5 %multiply_reduce_fusion.1 = (f32[2048]{0:T(1024)S(1)}, f32[2048]{0:T(1024)S(1)}, f32[1024,2048]{1,0:T(8,128)}) fusion(f32[1024]{0:T(1024)S(1)} %bitcast.109, bf16[1024,1024]{0,1:T(8,128)(2,1)S(1)} %bitcast.85, bf16[1024,2048]{0,1:T(8,128)(2,1)} %all-gather.7.cloned.1.call-done), kind=kOutput, calls=%fused_computation.19 | convolution fusion | flops 4318031872 | bytes 14700544 | tf_op jit(solution)/shard_map/dot_general | solution.py:156
  158.5 39.1 %all-reduce.6 = (f32[2,2048]{1,0:T(2,128)S(1)}, f32[]{:T(128)}) all-reduce(f32[2,2048]{1,0:T(2,128)S(1)} %pad_maximum_fusion.3, f32[]{:T(128)} %get-tuple-element.151), channel_id=1, replica_groups=mesh['ids'=8,'mdl'=4] {'ids','mdl'}, use_global_device_ids=true, to_apply=%region_2.3 | all-reduce | flops 4097 | bytes 32776 | tf_op jit(solution)/shard_map/psum | solution.py:160
  198.9 7.3 add_convert_fusion.1
  206.2 18.3 %multiply_reduce_fusion = (f32[2048]{0:T(1024)S(1)}, f32[2048]{0:T(1024)S(1)}, f32[1024,2048]{1,0:T(8,128)}, f32[1024,2048]{1,0:T(8,128)}) fusion(f32[1024]{0:T(1024)S(1)} %bitcast.110, bf16[1024,2048]{1,0:T(8,128)(2,1)} %add_convert_fusion.1, bf16[2048,2048]{0,1:T(8,128)(2,1)} %all-gather.11.cloned.1.call-done), kind=kOutput, calls=%fused_computation.17 | convolution fusion | flops 8612999168 | bytes 29380608 | tf_op jit(solution)/shard_map/dot_general | solution.py:165
  224.5 40.1 %psum.58 = f32[2,2048]{1,0:T(2,128)S(1)} all-reduce(f32[2,2048]{1,0:T(2,128)S(1)} %pad_maximum_fusion.4), channel_id=1, replica_groups=mesh['ids'=8,'mdl'=4] {'ids','mdl'}, use_global_device_ids=true, to_apply=%region_7.8 | all-reduce | flops 4096 | bytes 32768 | tf_op jit(solution)/shard_map/psum | solution.py:168
  274.9 40.2 %psum.59 = f32[2,2048]{1,0:T(2,128)S(1)} all-reduce(f32[2,2048]{1,0:T(2,128)S(1)} %pad_maximum_fusion.5), channel_id=1, replica_groups=mesh['ids'=8,'mdl'=4] {'ids','mdl'}, use_global_device_ids=true, to_apply=%region_10.11 | all-reduce | flops 4096 | bytes 32768 | tf_op jit(solution)/shard_map/psum | solution.py:198
  315.1 12.7 %multiply_convert_fusion.1 = bf16[1024,2048]{1,0:T(8,128)(2,1)S(1)} fusion(f32[1024,2048]{1,0:T(8,128)} %get-tuple-element.167, f32[1024,2048]{1,0:T(8,128)} %get-tuple-element.165, f32[1024,2048]{1,0:T(8,128)} %get-tuple-element.148, f32[]{:T(128)} %get-tuple-element.125, f32[2048]{0:T(1024)S(1)} %bitcast.120, f32[2048]{0:T(1024)S(1)} %bitcast.119, ...), kind=kLoop, calls=%fused_computation.25 | loop fusion | flops 52428800 | bytes 29405188 | tf_op jit(solution)/shard_map/convert_element_type | solution.py:213
  327.8 18.4 %multiply_reduce_fusion.2 = (f32[2048]{0:T(1024)S(1)}, f32[2048]{0:T(1024)S(1)}, f32[1024,2048]{1,0:T(8,128)}) fusion(f32[2048]{0:T(1024)S(1)} %bitcast.94, f32[2048]{0:T(1024)S(1)} %bitcast.97, f32[1024,2048]{1,0:T(8,128)} %get-tuple-element.164, bf16[1024,2048]{1,0:T(8,128)(2,1)S(1)} %multiply_convert_fusion.1, ...), kind=kOutput, calls=%fused_computation.24 | convolution fusion | flops 8615096320 | bytes 29392896 | tf_op jit(solution)/shard_map/dot_general | solution.py:36
  346.2 40.7 %all-reduce.5 = (f32[2,2048]{1,0:T(2,128)S(1)}, f32[32]{0:T(128)S(1)}) all-reduce(f32[2,2048]{1,0:T(2,128)S(1)} %pad_maximum_fusion.6, f32[32]{0:T(128)S(1)} %get-tuple-element.144), channel_id=1, replica_groups=mesh['ids'=8,'mdl'=4] {'ids','mdl'}, use_global_device_ids=true, to_apply=%region_13.14 | all-reduce | flops 4128 | bytes 33024 | tf_op jit(solution)/shard_map/psum | solution.py:224
  386.9 11.3 %multiply_convert_fusion = bf16[1024,2048]{1,0:T(8,128)(2,1)S(1)} fusion(f32[1024,2048]{1,0:T(8,128)} %get-tuple-element.168, f32[1024,2048]{1,0:T(8,128)} %get-tuple-element.164, f32[2048]{0:T(1024)S(1)} %bitcast.114, f32[2048]{0:T(1024)S(1)} %bitcast.113, f32[]{:T(128)} %get-tuple-element.125, f32[2048]{0:T(1024)S(1)} %bitcast.95, f32[2048]{0:T(1024)S(1)} %bitcast.98, ...), kind=kLoop, calls=%fused_computation.23 | loop fusion | flops 54525952 | bytes 21016580 | tf_op jit(solution)/shard_map/convert_element_type | solution.py:242
  419.4 6.5 pad_maximum_fusion
  431.8 47.1 %reduce-scatter.4.cloned.1.call-done = f32[1,1024,512]{2,1,0:T(8,128)} async-done(((f32[4,1024,512]{2,1,0:T(8,128)}), f32[1,1024,512]{2,1,0:T(8,128)}) %reduce-scatter.4.cloned.1.call-update) | async-done | bytes 2097168 | tf_op jit(solution)/shard_map/reduce_scatter | solution.py:249
  479.0 127.4 %reduce-scatter.8.cloned.1.call-done = f32[1,2048,512]{2,1,0:T(8,128)} async-done(((f32[4,2048,512]{2,1,0:T(8,128)}), f32[1,2048,512]{2,1,0:T(8,128)}) %reduce-scatter.8.cloned.1.call-update) | async-done | bytes 4194320 | tf_op jit(solution)/shard_map/reduce_scatter | solution.py:220
  613.7 6.8 fusion.18
  630.0 109.6 %all-reduce.12.cloned.1.call-done = f32[2048,32]{0,1:T(8,128)} async-done(((f32[2048,32]{0,1:T(8,128)}), f32[2048,32]{0,1:T(8,128)}) %all-reduce.12.cloned.1.call-update) | async-done | bytes 262160 | tf_op jit(solution)/shard_map/psum | solution.py:224
  742.6 15.7 %all_gather.34 = bf16[8,1024,32]{2,1,0:T(8,128)(2,1)S(1)} all-gather(bf16[8,256,32]{2,1,0:T(8,128)(2,1)S(1)} %reshape.98), channel_id=1, replica_groups=mesh['ids'=8,'mdl'=4] {'mdl'}, dimensions={1}, use_global_device_ids=true | all-gather | bytes 655360 | tf_op jit(solution)/shard_map/all_gather | solution.py:185
  758.3 14.1 %fusion.19 = bf16[2048,32]{0,1:T(8,128)(2,1)S(1)} fusion(bf16[8192,32]{1,0:T(8,128)(2,1)S(1)} %bitcast.83, s32[2048]{0:T(1024)S(1)} %dynamic-slice-done), kind=kOutput, calls=%fused_computation.48 | convolution fusion | flops 1090584576 | bytes 663552 | tf_op jit(solution)/shard_map/dot_general | solution.py:192
  772.4 7.5 all_gather.35
  779.9 30.7 %reduce-scatter.6.cloned.1.call-done = f32[128,512]{1,0:T(8,128)} async-done(((f32[1024,512]{1,0:T(8,128)}), f32[128,512]{1,0:T(8,128)}) %reduce-scatter.6.cloned.1.call-update) | async-done | bytes 262160 | tf_op jit(solution)/shard_map/reduce_scatter | solution.py:250
  815.0 154.8 %all-reduce.10.cloned.1.call-done = f32[4,512,512]{2,1,0:T(8,128)} async-done(((f32[4,512,512]{2,1,0:T(8,128)}), f32[4,512,512]{2,1,0:T(8,128)}) %all-reduce.10.cloned.1.call-update) | async-done | bytes 4194320 | tf_op jit(solution)/shard_map/psum | solution.py:221
  983.5 9.0 fusion.48
  (156 shorter events, 135.5 us)
Async XLA Ops:
  7.2 46.1 %all-gather.5.cloned.1.call-start = ((), (), s32[]{:S(2)}) async-start(), calls=%async_computation.7 | async-start | bytes 1179648 | tf_op jit(solution)/shard_map/all_gather | solution.py:109
  9.0 129.6 %all-gather.9.cloned.1.call-start = ((), (), s32[]{:S(2)}) async-start(), calls=%async_computation.9 | async-start | bytes 1310720 | tf_op jit(solution)/shard_map/all_gather | solution.py:142
  48.2 98.8 %all-gather.7.cloned.1.call-start = ((), (), s32[]{:S(2)}) async-start(), calls=%async_computation.8 | async-start | bytes 5242880 | tf_op jit(solution)/shard_map/all_gather | solution.py:110
  53.3 152.9 %all-gather.11.cloned.1.call-start = ((), (), s32[]{:S(2)}) async-start(), calls=%async_computation.10 | async-start | bytes 10485760 | tf_op jit(solution)/shard_map/all_gather | solution.py:115
  66.3 11.7 %all-to-all-start = ((s32[8,1,1024]{2,1,0:T(1,128)}), s32[8,1,1024]{2,1,0:T(1,128)S(1)}, u32[]{:S(2)}, u32[]{:S(2)}) async-start(s32[8,1,1024]{2,1,0:T(1,128)} %all_to_all.32), calls=%async_computation | async-start | bytes 65536 | tf_op jit(solution)/shard_map/all_to_all | solution.py:127
  78.0 68.4 %copy-start.12 = (s32[8,1,1024]{2,1,0:T(1,128)}, s32[8,1,1024]{2,1,0:T(1,128)S(1)}, u32[]{:S(2)}) copy-start(s32[8,1,1024]{2,1,0:T(1,128)S(1)} %all-to-all-done) | copy-start | bytes 98308
  78.0 58.2 %all-to-all-start.1 = ((bf16[4,1024,256]{2,1,0:T(8,128)(2,1)}), bf16[4,1024,256]{2,1,0:T(8,128)(2,1)S(1)}, u32[]{:S(2)}, u32[]{:S(2)}) async-start(bf16[4,1024,256]{2,1,0:T(8,128)(2,1)} %bitcast.3), calls=%async_computation.1 | async-start | bytes 4194304 | tf_op jit(solution)/shard_map/all_to_all | solution.py:120
  81.6 397.3 %reduce-scatter.4.cloned.1.call-start = ((), (), s32[]{:S(2)}) async-start(), calls=%async_computation.11 | async-start | bytes 10485760 | tf_op jit(solution)/shard_map/reduce_scatter | solution.py:249
  206.2 59.3 %copy-start.21 = (f32[32]{0:T(128)S(1)}, f32[32]{0:T(128)}, u32[]{:S(2)}) copy-start(f32[32]{0:T(128)} %param.29) | copy-start | bytes 388
  406.9 199.5 %reduce-scatter.8.cloned.1.call-start = ((), (), s32[]{:S(2)}) async-start(), calls=%async_computation.13 | async-start | bytes 20971520 | tf_op jit(solution)/shard_map/reduce_scatter | solution.py:220
  426.0 180.5 %copy-start.7 = (f32[128,450]{0,1:T(8,128)S(1)}, f32[128,450]{0,1:T(8,128)}, u32[]{:S(2)}) copy-start(f32[128,450]{0,1:T(8,128)} %param.25) | copy-start | bytes 691204
  426.0 180.7 %copy-start.10 = (f32[128,450]{0,1:T(8,128)S(1)}, f32[128,450]{0,1:T(8,128)}, u32[]{:S(2)}) copy-start(f32[128,450]{0,1:T(8,128)} %param.31) | copy-start | bytes 691204
  426.0 180.8 %copy-start.11 = (f32[128,450]{0,1:T(8,128)S(1)}, f32[128,450]{0,1:T(8,128)}, u32[]{:S(2)}) copy-start(f32[128,450]{0,1:T(8,128)} %param.30) | copy-start | bytes 691204
  426.0 313.6 %all-reduce.12.cloned.1.call-start = ((), (), s32[]{:S(2)}) async-start(), calls=%async_computation.15 | async-start | bytes 524288 | tf_op jit(solution)/shard_map/psum | solution.py:224
  431.8 378.8 %reduce-scatter.6.cloned.1.call-start = ((), (), s32[]{:S(2)}) async-start(), calls=%async_computation.12 | async-start | bytes 2359296 | tf_op jit(solution)/shard_map/reduce_scatter | solution.py:250
  478.9 490.8 %all-reduce.10.cloned.1.call-start = ((), (), s32[]{:S(2)}) async-start(), calls=%async_computation.14 | async-start | bytes 8388608 | tf_op jit(solution)/shard_map/psum | solution.py:221
  606.6 22.7 %copy-start.16 = (f32[4,450]{1,0:T(4,128)S(1)}, f32[4,450]{1,0:T(4,128)}, u32[]{:S(2)}) copy-start(f32[4,450]{1,0:T(4,128)} %param.28) | copy-start | bytes 21604
  606.6 22.7 %copy-start.18 = (f32[4,450]{1,0:T(4,128)S(1)}, f32[4,450]{1,0:T(4,128)}, u32[]{:S(2)}) copy-start(f32[4,450]{1,0:T(4,128)} %param.37) | copy-start | bytes 21604
  606.6 22.7 %copy-start.19 = (f32[4,450]{1,0:T(4,128)S(1)}, f32[4,450]{1,0:T(4,128)}, u32[]{:S(2)}) copy-start(f32[4,450]{1,0:T(4,128)} %param.36) | copy-start | bytes 21604
  606.7 133.0 %copy-start.9 = (f32[450,32]{0,1:T(8,128)S(1)}, f32[450,32]{0,1:T(8,128)}, u32[]{:S(2)}) copy-start(f32[450,32]{0,1:T(8,128)} %param.27) | copy-start | bytes 172804
  606.7 133.0 %copy-start.13 = (f32[450,32]{0,1:T(8,128)S(1)}, f32[450,32]{0,1:T(8,128)}, u32[]{:S(2)}) copy-start(f32[450,32]{0,1:T(8,128)} %param.35) | copy-start | bytes 172804
  606.7 133.0 %copy-start.14 = (f32[450,32]{0,1:T(8,128)S(1)}, f32[450,32]{0,1:T(8,128)}, u32[]{:S(2)}) copy-start(f32[450,32]{0,1:T(8,128)} %param.34) | copy-start | bytes 172804
  613.7 144.6 %dynamic-slice-start = ((s32[8192]{0:T(1024)}, s32[]{:T(128)}), s32[2048]{0:T(1024)S(1)}, s32[]{:S(2)}) async-start(s32[8192]{0:T(1024)} %param.23, s32[]{:T(128)} %select_n.30), calls=%async_computation.16 | async-start | bytes 16896 | tf_op jit(solution)/shard_map/dynamic_slice | solution.py:187
  623.3 118.1 %all-to-all-start.3 = ((bf16[8,2,4096]{2,1,0:T(2,128)(2,1)}), bf16[8,2,4096]{2,1,0:T(2,128)(2,1)S(1)}, u32[]{:S(2)}, u32[]{:S(2)}) async-start(bf16[8,2,4096]{2,1,0:T(2,128)(2,1)} %reshape.109), calls=%async_computation.3 | async-start | bytes 262144 | tf_op jit(solution)/shard_map/all_to_all | solution.py:184
  (13 other events, 164.2 us)
Sparse Core Ops, SparseCore 0:
  10.6 42.5 all-gather.4
  55.4 17.2 all-gather.8
  74.3 56.9 all-gather.6
  133.3 57.1 all-gather.10
  407.0 71.8 reduce-scatter.3
  481.3 125.0 reduce-scatter.7
  612.5 127.0 all-reduce.11
  743.2 67.4 reduce-scatter.5
  814.3 155.4 all-reduce.9
where the time goes:
time: 1010 us; the launch traced here: 1000 us
  waiting for transfers between devices  477 us (47%)
  blocking collectives  262 us (26%)
  matrix products  121 us (12%)
  other arithmetic  72.2 us (7%)
  local copies, waits for them, and re-layouts  37.4 us (4%)
  between operations  15.7 us (2%)
  starting transfers between devices  15 us (1%)
    psum x1, waiting for transfers between devices, body(): grad_second = lax.psum(grad_second, 'ids')  155 us
    reduce_scatter x1, waiting for transfers between devices, body(): lax.psum_scatter(local_second, 'mdl', scatter_dimension=0, tiled=False)  127 us
    psum x1, waiting for transfers between devices, body(): lax.psum((jnp.stack([jnp.sum(incoming_one * unit_one, 0), jnp.sum(incomin...  110 us
    all_gather x1, blocking collectives, body(): lax.all_gather(jnp.pad(norm_params, ((0, 0), (0, more))), 'mdl', axis=1,...  48.9 us
    reduce_scatter x1, waiting for transfers between devices, body(): lax.psum_scatter(local_first, 'mdl', scatter_dimension=0, tiled=False)  47.1 us
    dot_general x11, matrix products, contract(): lax.dot_general(left, right, (((left_dim,), (right_dim,)), ((), ())), pre...  45.5 us
    psum x1, blocking collectives, body(): lax.psum((jnp.stack([jnp.sum(incoming_one * unit_one, 0), jnp.sum(incomin...  40.7 us
    psum x1, blocking collectives, body(): lax.psum(jnp.stack([jnp.sum(incoming_two * unit_two, 0), jnp.sum(incoming...  40.2 us
  transfers between devices with their start and end apart: 12, of which 7 were waited for; matrix products, arithmetic and copies ran while one was open for 12% of the time, Pallas kernels for 0%

commit v1 on v0

--- a/solution.py
+++ b/solution.py
@@ -14,6 +14,15 @@
 rate_norm = 0.5
 rate_bias = 0.02
 LANES = 128
+
+
+def sum_by_hops(x, mesh_axis):
+    devices = lax.axis_size(mesh_axis)
+    acc, hop = (x, 1)
+    while hop < devices:
+        acc = acc + lax.ppermute(acc, mesh_axis, [(i, i ^ hop) for i in range(devices)])
+        hop = 2 * hop
+    return acc
 
 
 def mish_parts(inputs):
@@ -218,7 +227,7 @@
         ]
     )
     grad_second = lax.psum_scatter(local_second, "mdl", scatter_dimension=0, tiled=False)
-    grad_second = lax.psum(grad_second, "ids")
+    grad_second = sum_by_hops(grad_second, "ids")
     grad_second = grad_second.reshape(parts, wide, wide)[:, :width, :width].reshape(-1, width)
     incoming_one = contract(grad_linear_two, second_low, 1, 1)
     sums_one, final_sum, grad_bias = lax.psum(

time: 1010 us -> 972 us (0.962)
  waiting for transfers between devices: 477 us -> 423 us
  other arithmetic: 72.2 us -> 88.1 us
    ppermute x0 -> x3, waiting for transfers between devices: none -> 177 us  [sum_by_hops(): lax.ppermute(acc, mesh_axis, [(i, i ^ hop) for i in range(devices)])]
    psum x1 -> x0, waiting for transfers between devices: 155 us -> none  [body(): grad_second = lax.psum(grad_second, 'ids')]
    reduce_scatter x1, waiting for transfers between devices: 127 us -> 45.1 us  [body(): lax.psum_scatter(local_second, 'mdl', scatter_dimension=0, tiled=False)]
    psum x1, waiting for transfers between devices: 110 us -> 160 us  [body(): lax.psum((jnp.stack([jnp.sum(incoming_one * unit_one, 0), jnp.sum(incomin...]
    reduce_scatter x1, waiting for transfers between devices: 47.1 us -> 0.02 us  [body(): lax.psum_scatter(local_first, 'mdl', scatter_dimension=0, tiled=False)]
    add x0 -> x3, other arithmetic: none -> 16 us  [sum_by_hops(): acc + lax.ppermute(acc, mesh_axis, [(i, i ^ hop) for i in range(devices)])]
  transfers between devices with their start and end apart: 12 -> 14, of which waited for: 7 -> 7; matrix products, arithmetic and copies ran while one was open for 12% -> 16% of each run, Pallas kernels for 0% -> 0%
where the time goes in v1:
time: 972 us; the launch traced here: 963 us
  waiting for transfers between devices  423 us (44%)
  blocking collectives  263 us (27%)
  matrix products  118 us (12%)
  other arithmetic  88.1 us (9%)
  local copies, waits for them, and re-layouts  35.4 us (4%)
  starting transfers between devices  18.8 us (2%)
  between operations  15.9 us (2%)
    ppermute x3, waiting for transfers between devices, sum_by_hops(): lax.ppermute(acc, mesh_axis, [(i, i ^ hop) for i in range(devices)])  177 us
    psum x1, waiting for transfers between devices, body(): lax.psum((jnp.stack([jnp.sum(incoming_one * unit_one, 0), jnp.sum(incomin...  160 us
    all_gather x1, blocking collectives, body(): lax.all_gather(jnp.pad(norm_params, ((0, 0), (0, more))), 'mdl', axis=1,...  48.9 us
    reduce_scatter x1, waiting for transfers between devices, body(): lax.psum_scatter(local_second, 'mdl', scatter_dimension=0, tiled=False)  45.1 us
    dot_general x11, matrix products, contract(): lax.dot_general(left, right, (((left_dim,), (right_dim,)), ((), ())), pre...  43.2 us
    psum x1, blocking collectives, body(): lax.psum((jnp.stack([jnp.sum(incoming_one * unit_one, 0), jnp.sum(incomin...  41.6 us
    psum x1, blocking collectives, body(): lax.psum(jnp.stack([jnp.sum(incoming_two * unit_two, 0), jnp.sum(incoming...  40.4 us
    psum x1, blocking collectives, body(): lax.psum(jnp.stack([jnp.sum(weighted_two, 0), jnp.sum(weighted_two * acti...  40.1 us
  transfers between devices with their start and end apart: 14, of which 7 were waited for; matrix products, arithmetic and copies ran while one was open for 16% of the time, Pallas kernels for 0%

profile of v1, /device:TPU:0, one launch (start us, length us, event | category | flops | bytes accessed | tf_op | source)
XLA Modules:
  0.0 963.1 jit_solution(8352940345309662464)
XLA Ops:
  9.8 13.0 %subtract_convert_fusion = (bf16[2048,32]{0,1:T(8,128)(2,1)S(1)}, bf16[2048,32]{0,1:T(8,128)(2,1)S(1)}) fusion(bf16[8192,32]{0,1:T(8,128)(2,1)S(1)} %copy-done, s32[8192]{0:T(1024)S(1)} %fusion.37), kind=kOutput, calls=%fused_computation.68 | convolution fusion | flops 1090846720 | bytes 819200 | tf_op jit(solution)/shard_map/dot_general | solution.py:143
  26.4 18.5 %all_to_all.48 = bf16[8,2,8192]{2,1,0:T(2,128)(2,1)S(1)} all-to-all(bf16[8,2,8192]{2,1,0:T(2,128)(2,1)S(1)} %reshape.106), channel_id=1, replica_groups=mesh['ids'=8,'mdl'=4] {'ids'}, dimensions={0} | all-to-all | bytes 524288 | tf_op jit(solution)/shard_map/all_to_all | solution.py:150
  81.7 48.9 %all_gather.27 = f32[4,2048]{1,0:T(4,128)S(1)} all-gather(f32[4,512]{1,0:T(4,128)S(1)} %pad.17), channel_id=1, replica_groups=mesh['ids'=8,'mdl'=4] {'mdl'}, dimensions={1}, use_global_device_ids=true | all-gather | bytes 40960 | tf_op jit(solution)/shard_map/all_gather | solution.py:127
  147.0 11.5 %multiply_reduce_fusion.1 = (f32[2048]{0:T(1024)S(1)}, f32[2048]{0:T(1024)S(1)}, f32[1024,2048]{1,0:T(8,128)}) fusion(f32[1024]{0:T(1024)S(1)} %bitcast.112, bf16[1024,1024]{0,1:T(8,128)(2,1)S(1)} %bitcast.88, bf16[1024,2048]{0,1:T(8,128)(2,1)} %all-gather.7.cloned.1.call-done), kind=kOutput, calls=%fused_computation.19 | convolution fusion | flops 4318031872 | bytes 14700544 | tf_op jit(solution)/shard_map/dot_general | solution.py:165
  158.5 39.1 %all-reduce.6 = (f32[2,2048]{1,0:T(2,128)S(1)}, f32[]{:T(128)}) all-reduce(f32[2,2048]{1,0:T(2,128)S(1)} %pad_maximum_fusion.3, f32[]{:T(128)} %get-tuple-element.151), channel_id=1, replica_groups=mesh['ids'=8,'mdl'=4] {'ids','mdl'}, use_global_device_ids=true, to_apply=%region_2.3 | all-reduce | flops 4097 | bytes 32776 | tf_op jit(solution)/shard_map/psum | solution.py:169
  198.9 7.3 add_convert_fusion.1
  206.2 18.4 %multiply_reduce_fusion = (f32[2048]{0:T(1024)S(1)}, f32[2048]{0:T(1024)S(1)}, f32[1024,2048]{1,0:T(8,128)}, f32[1024,2048]{1,0:T(8,128)}) fusion(f32[1024]{0:T(1024)S(1)} %bitcast.113, bf16[1024,2048]{1,0:T(8,128)(2,1)} %add_convert_fusion.1, bf16[2048,2048]{0,1:T(8,128)(2,1)} %all-gather.11.cloned.1.call-done), kind=kOutput, calls=%fused_computation.17 | convolution fusion | flops 8612999168 | bytes 29380608 | tf_op jit(solution)/shard_map/dot_general | solution.py:174
  224.6 40.1 %psum.51 = f32[2,2048]{1,0:T(2,128)S(1)} all-reduce(f32[2,2048]{1,0:T(2,128)S(1)} %pad_maximum_fusion.4), channel_id=1, replica_groups=mesh['ids'=8,'mdl'=4] {'ids','mdl'}, use_global_device_ids=true, to_apply=%region_7.8 | all-reduce | flops 4096 | bytes 32768 | tf_op jit(solution)/shard_map/psum | solution.py:177
  275.0 40.4 %psum.52 = f32[2,2048]{1,0:T(2,128)S(1)} all-reduce(f32[2,2048]{1,0:T(2,128)S(1)} %pad_maximum_fusion.5), channel_id=1, replica_groups=mesh['ids'=8,'mdl'=4] {'ids','mdl'}, use_global_device_ids=true, to_apply=%region_10.11 | all-reduce | flops 4096 | bytes 32768 | tf_op jit(solution)/shard_map/psum | solution.py:207
  315.4 13.0 %multiply_convert_fusion.1 = bf16[1024,2048]{1,0:T(8,128)(2,1)S(1)} fusion(f32[1024,2048]{1,0:T(8,128)} %get-tuple-element.167, f32[1024,2048]{1,0:T(8,128)} %get-tuple-element.165, f32[1024,2048]{1,0:T(8,128)} %get-tuple-element.148, f32[]{:T(128)} %get-tuple-element.125, f32[2048]{0:T(1024)S(1)} %bitcast.123, f32[2048]{0:T(1024)S(1)} %bitcast.122, ...), kind=kLoop, calls=%fused_computation.25 | loop fusion | flops 52428800 | bytes 29405188 | tf_op jit(solution)/shard_map/convert_element_type | solution.py:222
  344.3 18.9 %multiply_reduce_fusion.2 = (f32[2048]{0:T(1024)S(1)}, f32[2048]{0:T(1024)S(1)}, f32[1024,2048]{1,0:T(8,128)}) fusion(f32[2048]{0:T(1024)S(1)} %bitcast.97, f32[2048]{0:T(1024)S(1)} %bitcast.100, f32[1024,2048]{1,0:T(8,128)} %get-tuple-element.164, bf16[1024,2048]{1,0:T(8,128)(2,1)} %copy-done.4, bf16[2048,2048]{0,1:T(8,128)(2,1)} %all-gather.11.cloned.1.call-done), kind=kOutput, calls=%fused_computation.24 | convolution fusion | flops 8615096320 | bytes 29392896 | tf_op jit(solution)/shard_map/dot_general | solution.py:45
  363.2 41.6 %all-reduce.5 = (f32[2,2048]{1,0:T(2,128)S(1)}, f32[32]{0:T(128)S(1)}) all-reduce(f32[2,2048]{1,0:T(2,128)S(1)} %pad_maximum_fusion.6, f32[32]{0:T(128)S(1)} %get-tuple-element.144), channel_id=1, replica_groups=mesh['ids'=8,'mdl'=4] {'ids','mdl'}, use_global_device_ids=true, to_apply=%region_13.14 | all-reduce | flops 4128 | bytes 33024 | tf_op jit(solution)/shard_map/psum | solution.py:233
  404.9 11.2 %multiply_convert_fusion = bf16[1024,2048]{1,0:T(8,128)(2,1)S(1)} fusion(f32[1024,2048]{1,0:T(8,128)} %get-tuple-element.168, f32[1024,2048]{1,0:T(8,128)} %get-tuple-element.164, f32[2048]{0:T(1024)S(1)} %bitcast.117, f32[2048]{0:T(1024)S(1)} %bitcast.116, f32[]{:T(128)} %get-tuple-element.125, f32[2048]{0:T(1024)S(1)} %bitcast.98, f32[2048]{0:T(1024)S(1)} %bitcast.101, ...), kind=kLoop, calls=%fused_computation.23 | loop fusion | flops 54525952 | bytes 21016580 | tf_op jit(solution)/shard_map/convert_element_type | solution.py:251
  424.8 45.1 %reduce-scatter.8.cloned.1.call-done = f32[1,2048,512]{2,1,0:T(8,128)} async-done(((f32[4,2048,512]{2,1,0:T(8,128)}), f32[1,2048,512]{2,1,0:T(8,128)}) %reduce-scatter.8.cloned.1.call-update) | async-done | bytes 4194320 | tf_op jit(solution)/shard_map/reduce_scatter | solution.py:229
  471.3 91.0 %collective-permute-done = f32[2048,512]{1,0:T(8,128)S(1)} collective-permute-done((f32[2048,512]{1,0:T(8,128)}, f32[2048,512]{1,0:T(8,128)S(1)}, u32[]{:S(2)}, u32[]{:S(2)}) %collective-permute-start) | collective-permute-done | bytes 4194336 | tf_op jit(solution)/shard_map/ppermute | solution.py:23
  575.3 85.8 %collective-permute-done.1 = f32[2048,512]{1,0:T(8,128)} collective-permute-done((f32[2048,512]{1,0:T(8,128)}, f32[2048,512]{1,0:T(8,128)}, u32[]{:S(2)}, u32[]{:S(2)}) %collective-permute-start.1) | collective-permute-done | bytes 4194336 | tf_op jit(solution)/shard_map/ppermute | solution.py:23
  661.1 6.4 add.278
  677.1 6.8 fusion.18
  691.8 159.9 %all-reduce.9.cloned.1.call-done = f32[2048,32]{0,1:T(8,128)} async-done(((f32[2048,32]{0,1:T(8,128)}), f32[2048,32]{0,1:T(8,128)}) %all-reduce.9.cloned.1.call-update) | async-done | bytes 262160 | tf_op jit(solution)/shard_map/psum | solution.py:233
  854.7 16.1 %all_gather.34 = bf16[8,1024,32]{2,1,0:T(8,128)(2,1)S(1)} all-gather(bf16[8,256,32]{2,1,0:T(8,128)(2,1)S(1)} %reshape.98), channel_id=1, replica_groups=mesh['ids'=8,'mdl'=4] {'mdl'}, dimensions={1}, use_global_device_ids=true | all-gather | bytes 655360 | tf_op jit(solution)/shard_map/all_gather | solution.py:194
  870.8 14.1 %fusion.19 = bf16[2048,32]{0,1:T(8,128)(2,1)S(1)} fusion(bf16[8192,32]{1,0:T(8,128)(2,1)S(1)} %bitcast.86, s32[2048]{0:T(1024)S(1)} %dynamic-slice-done), kind=kOutput, calls=%fused_computation.48 | convolution fusion | flops 1090584576 | bytes 663552 | tf_op jit(solution)/shard_map/dot_general | solution.py:201
  884.9 7.5 all_gather.35
  892.4 33.0 %reduce-scatter.6.cloned.1.call-done = f32[128,512]{1,0:T(8,128)} async-done(((f32[1024,512]{1,0:T(8,128)}), f32[128,512]{1,0:T(8,128)}) %reduce-scatter.6.cloned.1.call-update) | async-done | bytes 262160 | tf_op jit(solution)/shard_map/reduce_scatter | solution.py:259
  946.0 9.0 fusion.48
  (160 shorter events, 150.5 us)
Async XLA Ops:
  7.2 46.1 %all-gather.5.cloned.1.call-start = ((), (), s32[]{:S(2)}) async-start(), calls=%async_computation.7 | async-start | bytes 1179648 | tf_op jit(solution)/shard_map/all_gather | solution.py:118
  9.0 129.6 %all-gather.9.cloned.1.call-start = ((), (), s32[]{:S(2)}) async-start(), calls=%async_computation.9 | async-start | bytes 1310720 | tf_op jit(solution)/shard_map/all_gather | solution.py:151
  48.2 98.8 %all-gather.7.cloned.1.call-start = ((), (), s32[]{:S(2)}) async-start(), calls=%async_computation.8 | async-start | bytes 5242880 | tf_op jit(solution)/shard_map/all_gather | solution.py:119
  53.3 152.9 %all-gather.11.cloned.1.call-start = ((), (), s32[]{:S(2)}) async-start(), calls=%async_computation.10 | async-start | bytes 10485760 | tf_op jit(solution)/shard_map/all_gather | solution.py:124
  66.3 11.7 %all-to-all-start = ((s32[8,1,1024]{2,1,0:T(1,128)}), s32[8,1,1024]{2,1,0:T(1,128)S(1)}, u32[]{:S(2)}, u32[]{:S(2)}) async-start(s32[8,1,1024]{2,1,0:T(1,128)} %all_to_all.32), calls=%async_computation | async-start | bytes 65536 | tf_op jit(solution)/shard_map/all_to_all | solution.py:136
  78.0 68.4 %copy-start.11 = (s32[8,1,1024]{2,1,0:T(1,128)}, s32[8,1,1024]{2,1,0:T(1,128)S(1)}, u32[]{:S(2)}) copy-start(s32[8,1,1024]{2,1,0:T(1,128)S(1)} %all-to-all-done) | copy-start | bytes 98308
  78.0 58.2 %all-to-all-start.1 = ((bf16[4,1024,256]{2,1,0:T(8,128)(2,1)}), bf16[4,1024,256]{2,1,0:T(8,128)(2,1)S(1)}, u32[]{:S(2)}, u32[]{:S(2)}) async-start(bf16[4,1024,256]{2,1,0:T(8,128)(2,1)} %bitcast.3), calls=%async_computation.1 | async-start | bytes 4194304 | tf_op jit(solution)/shard_map/all_to_all | solution.py:129
  81.6 388.3 %reduce-scatter.8.cloned.1.call-start = ((), (), s32[]{:S(2)}) async-start(), calls=%async_computation.13 | async-start | bytes 20971520 | tf_op jit(solution)/shard_map/reduce_scatter | solution.py:229
  206.2 59.4 %copy-start.20 = (f32[32]{0:T(128)S(1)}, f32[32]{0:T(128)}, u32[]{:S(2)}) copy-start(f32[32]{0:T(128)} %param.29) | copy-start | bytes 388
  344.3 230.5 %reduce-scatter.4.cloned.1.call-start = ((), (), s32[]{:S(2)}) async-start(), calls=%async_computation.11 | async-start | bytes 10485760 | tf_op jit(solution)/shard_map/reduce_scatter | solution.py:258
  424.8 426.9 %all-reduce.9.cloned.1.call-start = ((), (), s32[]{:S(2)}) async-start(), calls=%async_computation.14 | async-start | bytes 524288 | tf_op jit(solution)/shard_map/psum | solution.py:233
  469.9 92.4 %collective-permute-start = (f32[2048,512]{1,0:T(8,128)}, f32[2048,512]{1,0:T(8,128)S(1)}, u32[]{:S(2)}, u32[]{:S(2)}) collective-permute-start(f32[2048,512]{1,0:T(8,128)} %bitcast.85), channel_id=1, source_target_pairs={{0,4},{4,0},{8,12},{12,8},{16,20},{20,16},{24,28},{28,24},{1,5},{5... | collective-permute-start | bytes 12582920 | tf_op jit(solution)/shard_map/ppermute | solution.py:23
  567.5 93.6 %collective-permute-start.1 = (f32[2048,512]{1,0:T(8,128)}, f32[2048,512]{1,0:T(8,128)}, u32[]{:S(2)}, u32[]{:S(2)}) collective-permute-start(f32[2048,512]{1,0:T(8,128)} %bitcast_add_fusion), channel_id=1, source_target_pairs={{0,8},{4,12},{8,0},{12,4},{16,24},{20,28},{24,16},{28,20},{1,9},{5... | collective-permute-start | bytes 12582920 | tf_op jit(solution)/shard_map/ppermute | solution.py:23
  574.5 95.6 %copy-start.6 = (f32[128,450]{0,1:T(8,128)S(1)}, f32[128,450]{0,1:T(8,128)}, u32[]{:S(2)}) copy-start(f32[128,450]{0,1:T(8,128)} %param.25) | copy-start | bytes 691204
  574.5 95.9 %copy-start.9 = (f32[128,450]{0,1:T(8,128)S(1)}, f32[128,450]{0,1:T(8,128)}, u32[]{:S(2)}) copy-start(f32[128,450]{0,1:T(8,128)} %param.31) | copy-start | bytes 691204
  574.5 96.0 %copy-start.10 = (f32[128,450]{0,1:T(8,128)S(1)}, f32[128,450]{0,1:T(8,128)}, u32[]{:S(2)}) copy-start(f32[128,450]{0,1:T(8,128)} %param.30) | copy-start | bytes 691204
  574.5 350.9 %reduce-scatter.6.cloned.1.call-start = ((), (), s32[]{:S(2)}) async-start(), calls=%async_computation.12 | async-start | bytes 2359296 | tf_op jit(solution)/shard_map/reduce_scatter | solution.py:259
  667.5 262.3 %collective-permute-start.2 = (f32[2048,512]{1,0:T(8,128)}, f32[2048,512]{1,0:T(8,128)}, u32[]{:S(2)}, u32[]{:S(2)}) collective-permute-start(f32[2048,512]{1,0:T(8,128)} %add.278), channel_id=1, source_target_pairs={{0,16},{4,20},{8,24},{12,28},{16,0},{20,4},{24,8},{28,12},{1,17},{... | collective-permute-start | bytes 12582920 | tf_op jit(solution)/shard_map/ppermute | solution.py:23
  670.3 20.8 %copy-start.15 = (f32[4,450]{1,0:T(4,128)S(1)}, f32[4,450]{1,0:T(4,128)}, u32[]{:S(2)}) copy-start(f32[4,450]{1,0:T(4,128)} %param.28) | copy-start | bytes 21604
  670.3 181.4 %copy-start.8 = (f32[450,32]{0,1:T(8,128)S(1)}, f32[450,32]{0,1:T(8,128)}, u32[]{:S(2)}) copy-start(f32[450,32]{0,1:T(8,128)} %param.27) | copy-start | bytes 172804
  670.3 181.4 %copy-start.12 = (f32[450,32]{0,1:T(8,128)S(1)}, f32[450,32]{0,1:T(8,128)}, u32[]{:S(2)}) copy-start(f32[450,32]{0,1:T(8,128)} %param.35) | copy-start | bytes 172804
  670.3 181.4 %copy-start.13 = (f32[450,32]{0,1:T(8,128)S(1)}, f32[450,32]{0,1:T(8,128)}, u32[]{:S(2)}) copy-start(f32[450,32]{0,1:T(8,128)} %param.34) | copy-start | bytes 172804
  677.1 193.6 %dynamic-slice-start = ((s32[8192]{0:T(1024)}, s32[]{:T(128)}), s32[2048]{0:T(1024)S(1)}, s32[]{:S(2)}) async-start(s32[8192]{0:T(1024)} %param.23, s32[]{:T(128)} %select_n.30), calls=%async_computation.15 | async-start | bytes 16896 | tf_op jit(solution)/shard_map/dynamic_slice | solution.py:196
  686.7 166.7 %all-to-all-start.3 = ((bf16[8,2,4096]{2,1,0:T(2,128)(2,1)}), bf16[8,2,4096]{2,1,0:T(2,128)(2,1)S(1)}, u32[]{:S(2)}, u32[]{:S(2)}) async-start(bf16[8,2,4096]{2,1,0:T(2,128)(2,1)} %reshape.108), calls=%async_computation.3 | async-start | bytes 262144 | tf_op jit(solution)/shard_map/all_to_all | solution.py:193
  (14 other events, 193.8 us)
Sparse Core Ops, SparseCore 0:
  10.6 42.5 all-gather.4
  55.4 17.2 all-gather.8
  74.3 56.9 all-gather.6
  133.3 57.1 all-gather.10
  344.4 125.4 reduce-scatter.7
  472.4 71.3 reduce-scatter.3
  574.6 277.0 all-reduce.8
  855.2 70.1 reduce-scatter.5
